TPU v7x, 32 devices: a whole 2x2x4 slice. The times are simulated.
32 devices in a mesh: row: 16 (over z, y, x), col: 2 (over core).
Axes of the slice: x: 2, y: 2, z: 4, core: 2. Of those that a mesh axis runs over, the one named last changes fastest.
Arguments:
- matrix: float32 [4096, 4096], P('row', 'col'), may hold values from -15.625 to 15.625
Outputs:
- r_top: float32 [512, 4096], P(None, 'col')
- basis: float32 [4096, 512], P('row')
All inputs are finite; a program needn't handle non-finite values.
Results may differ from a plain program's by a relative error of at most 0.0003.
Values sent between devices are 32-bit elements; how exact they have to be, the bound alone decides.
A program may use at most 64 MiB of HBM per device.

v0:
```python
import math
import jax
import jax.numpy as jnp
from jax import lax
from jax.sharding import PartitionSpec as P

PANEL = 256


def spread(value, axis, source):
    kept = jnp.where(lax.axis_index(axis) == source, value, 0).astype(value.dtype)
    return lax.psum(kept, axis)


def inner(left, right):
    return lax.dot_general(
        left,
        right,
        (((0,), (0,)), ((), ())),
        precision=lax.Precision.HIGHEST,
        preferred_element_type=jnp.float32,
    )


def product(left, right):
    return jnp.dot(left, right, precision=lax.Precision.HIGHEST, preferred_element_type=jnp.float32)


def factor(gram, valid):
    width = gram.shape[0]
    identity = jnp.eye(width, dtype=jnp.float32)
    safe_gram = jnp.where(valid, gram, identity)
    lower_factor = jnp.linalg.cholesky(safe_gram)
    lower_inverse = lax.linalg.triangular_solve(lower_factor, identity, left_side=True, lower=True)
    return (lower_factor.T, lower_inverse.T)


def body(matrix):
    panel_cols = PANEL
    rows_all = matrix.shape[0] * lax.axis_size("row")
    holder = lax.axis_index("col") == 0
    panels = matrix[:, : 2 * panel_cols]
    first_panel = panels[:, :panel_cols]
    second_panel = panels[:, panel_cols:]
    first_gram = lax.psum(inner(first_panel, first_panel), "row")
    upper_first, inverse_first = factor(first_gram, holder)
    basis_first = product(first_panel, inverse_first)
    basis_first = spread(basis_first, "col", 0)
    local_terms = inner(basis_first, matrix)
    summed, panel_gram = lax.psum((local_terms, inner(second_panel, second_panel)), "row")
    coupling = summed[:, panel_cols : 2 * panel_cols]
    remainder = matrix - product(basis_first, summed)
    second_updated = remainder[:, panel_cols : 2 * panel_cols]
    second_gram = panel_gram - inner(coupling, coupling)
    upper_second, inverse_second = factor(second_gram, holder)
    basis_second = product(second_updated, inverse_second)
    basis_second = spread(basis_second, "col", 0)
    second_proj = lax.psum(inner(basis_second, remainder), "row")
    zeros = jnp.zeros((panel_cols, panel_cols), jnp.float32)
    first_rows = jnp.where(
        holder, jnp.concatenate([upper_first, summed[:, panel_cols:]], axis=1), summed
    )
    second_rows = jnp.where(
        holder,
        jnp.concatenate([zeros, upper_second, second_proj[:, 2 * panel_cols :]], axis=1),
        second_proj,
    )
    top = jnp.concatenate([first_rows, second_rows], axis=0)
    basis = jnp.concatenate([basis_first, basis_second], axis=1) * math.sqrt(rows_all)
    return (top, basis)


def solution(mesh):
    return jax.shard_map(
        body,
        mesh=mesh,
        in_specs=(P("row", "col"),),
        out_specs=(P(None, "col"), P("row", None)),
        check_vma=False,
    )
```

profile of v0, /device:TPU:1, one launch (start us, length us, event | category | flops | bytes accessed | tf_op | source)
XLA Modules:
  0.0 589.3 jit_solution(6052217583035175400)
XLA Ops:
  7.2 0.0 all-reduce.8.cloned.1.call-start
  7.2 2.3 fusion.18
  9.6 0.0 all-reduce.10.cloned.1.call-start
  9.7 111.9 %all-reduce.8.cloned.1.call-done = f32[256,256]{0,1:T(8,128)} async-done(((f32[256,256]{0,1:T(8,128)}), f32[256,256]{0,1:T(8,128)}) %all-reduce.8.cloned.1.call-update) | async-done | bytes 262160 | tf_op jit(solution)/shard_map/psum | solution.py:45
  121.6 0.1 copy.4
  121.7 0.1 fusion.11
  121.8 11.7 %cholesky.130 = f32[128,128]{1,0:T(8,128)S(1)} custom-call(f32[128,128]{1,0:T(8,128)S(1)} %cholesky.194), custom_call_target="Cholesky" | custom-call | tf_op jit(solution)/shard_map/jit(cholesky)/cholesky | solution.py:33
  133.6 9.8 %custom-call.13 = f32[1,128,128]{1,2,0:T(8,128)S(1)} custom-call(f32[1,128,128]{2,1,0:T(8,128)S(1)} %get-tuple-element.55), custom_call_target="InvertDiagBlocksLowerTriangular" | custom-call | tf_op jit(solution)/shard_map/jit(cholesky)/cholesky | solution.py:33
  143.4 0.2 constant_dynamic-update-slice_fusion.3
  143.6 0.3 convolution_subtract_fusion.5
  143.9 11.7 %cholesky.147 = f32[128,128]{1,0:T(8,128)S(1)} custom-call(f32[128,128]{1,0:T(8,128)S(1)} %convolution_subtract_fusion.5), custom_call_target="Cholesky" | custom-call | tf_op jit(solution)/shard_map/jit(cholesky)/cholesky | solution.py:33
  155.7 0.6 compare_reduce_fusion.2
  157.6 0.1 broadcast.93
  157.6 15.5 %while.4 = (s32[]{:T(128)}, f32[256,256]{1,0:T(8,128)S(1)}, s32[2,2]{1,0:T(2,128)S(1)}, f32[2,128,128]{2,1,0:T(8,128)S(1)}, s32[]{:T(128)}) while((s32[]{:T(128)}, f32[256,256]{1,0:T(8,128)S(1)}, s32[2,2]{1,0:T(2,128)S(1)}, f32[2,128,128]{2,1,0:T(8,128)S(1)}, s32[]{:T(128)}) %tuple.50), condition=%wide.while_cond, body=%wide.while_body.sunk | while | flops 2 | bytes 131189 | solution.py:34
  169.4 0.6 fusion.59
  170.0 1.3 bitcast_dynamic-update-slice_fusion.4
  171.3 0.6 fusion.59
  171.9 1.3 bitcast_dynamic-update-slice_fusion.4
  173.2 19.7 %custom-call.14 = f32[2,128,128]{1,2,0:T(8,128)S(1)} custom-call(f32[2,128,128]{2,1,0:T(8,128)S(1)} %get-tuple-element.18), custom_call_target="InvertDiagBlocksLowerTriangular" | custom-call | tf_op jit(solution)/shard_map/triangular_solve/custom-call.0 | solution.py:34
  192.9 0.3 fusion.25
  193.2 0.4 convolution_subtract_fusion.3
  193.6 0.3 fusion.32
  193.9 1.1 fusion.1
  195.1 0.0 all-reduce.16.cloned.1.call-start
  195.1 1.3 fusion.14
  196.4 20.3 %all-reduce.10.cloned.1.call-done = f32[256,256]{0,1:T(8,128)} async-done(((f32[256,256]{0,1:T(8,128)}), f32[256,256]{0,1:T(8,128)}) %all-reduce.10.cloned.1.call-update) | async-done | bytes 262160 | tf_op jit(solution)/shard_map/psum | solution.py:12
  216.8 4.2 fusion.41
  221.0 0.0 all-reduce.12.cloned.1.call-start
  221.0 134.4 %all-reduce.16.cloned.1.call-done = (f32[256,2048]{1,0:T(8,128)}, f32[256,256]{0,1:T(8,128)}) async-done(((f32[256,2048]{1,0:T(8,128)}, f32[256,256]{0,1:T(8,128)}), (f32[256,2048]{1,0:T(8,128)}, f32[256,256]{0,1:T(8,128)})) %all-reduce.16.cloned.1.call-update) | async-done | bytes 2359312 | tf_op jit(solution)/shard_map/psum | solution.py:50
  355.4 1.7 fusion
  357.1 0.1 copy.9
  357.3 11.7 %cholesky.164 = f32[128,128]{1,0:T(8,128)S(1)} custom-call(f32[128,128]{1,0:T(8,128)S(1)} %cholesky.197), custom_call_target="Cholesky" | custom-call | tf_op jit(solution)/shard_map/jit(cholesky)/cholesky | solution.py:33
  369.1 0.6 compare_reduce_fusion.1
  369.7 9.8 %custom-call.15 = f32[1,128,128]{1,2,0:T(8,128)S(1)} custom-call(f32[1,128,128]{2,1,0:T(8,128)S(1)} %get-tuple-element.51), custom_call_target="InvertDiagBlocksLowerTriangular" | custom-call | tf_op jit(solution)/shard_map/jit(cholesky)/cholesky | solution.py:33
  379.6 0.2 constant_dynamic-update-slice_fusion.1
  379.8 0.3 convolution_subtract_fusion.4
  380.0 11.7 %cholesky.181 = f32[128,128]{1,0:T(8,128)S(1)} custom-call(f32[128,128]{1,0:T(8,128)S(1)} %convolution_subtract_fusion.4), custom_call_target="Cholesky" | custom-call | tf_op jit(solution)/shard_map/jit(cholesky)/cholesky | solution.py:33
  391.8 0.6 compare_reduce_fusion
  393.7 0.7 fusion.22
  394.5 4.1 while.5
  394.7 0.6 fusion.60
  395.3 1.4 bitcast_dynamic-update-slice_fusion.5
  396.7 0.6 fusion.60
  397.3 1.4 bitcast_dynamic-update-slice_fusion.5
  398.6 19.7 %custom-call.16 = f32[2,128,128]{1,2,0:T(8,128)S(1)} custom-call(f32[2,128,128]{2,1,0:T(8,128)S(1)} %get-tuple-element.19), custom_call_target="InvertDiagBlocksLowerTriangular" | custom-call | tf_op jit(solution)/shard_map/triangular_solve/custom-call.0 | solution.py:34
  418.3 0.3 fusion.23
  418.6 0.4 convolution_subtract_fusion.2
  419.0 0.3 fusion.28
  419.4 3.5 convolution_subtract_fusion
  422.9 1.3 copy-done.2
  424.2 1.1 convolution_select_fusion
  425.4 0.0 all-reduce.14.cloned.1.call-start
  425.4 18.0 %all-reduce.12.cloned.1.call-done = f32[256,256]{0,1:T(8,128)} async-done(((f32[256,256]{0,1:T(8,128)}), f32[256,256]{0,1:T(8,128)}) %all-reduce.12.cloned.1.call-update) | async-done | bytes 262160 | tf_op jit(solution)/shard_map/psum | solution.py:12
  443.4 4.9 fusion.42
  448.3 0.1 copy.6
  448.4 1.4 slice.98
  449.8 0.1 copy.12
  450.0 3.1 maximum_select_fusion
  453.1 1.0 copy.13
  454.1 122.1 %all-reduce.14.cloned.1.call-done = f32[256,2048]{1,0:T(8,128)} async-done(((f32[256,2048]{1,0:T(8,128)}), f32[256,2048]{1,0:T(8,128)}) %all-reduce.14.cloned.1.call-update) | async-done | bytes 2097168 | tf_op jit(solution)/shard_map/psum | solution.py:58
  576.3 1.4 slice-done
  577.7 2.0 maximum_select_fusion.1
  579.7 0.2 copy-done.3
  579.9 2.5 pad_maximum_fusion
  (39 shorter events, 0.5 us)
Async XLA Ops:
  7.2 114.4 %all-reduce.8.cloned.1.call-start = ((), (), s32[]{:S(2)}) async-start(), calls=%async_computation | async-start | bytes 524288 | tf_op jit(solution)/shard_map/psum | solution.py:45
  9.6 207.2 %all-reduce.10.cloned.1.call-start = ((), (), s32[]{:S(2)}) async-start(), calls=%async_computation.1 | async-start | bytes 524288 | tf_op jit(solution)/shard_map/psum | solution.py:12
  121.8 72.1 %copy-start.1 = (f32[256,2048]{1,0:T(8,128)S(1)}, f32[256,2048]{1,0:T(8,128)}, u32[]{:S(2)}) copy-start(f32[256,2048]{1,0:T(8,128)} %param.4) | copy-start | bytes 6291460
  195.1 160.3 %all-reduce.16.cloned.1.call-start = ((), (), s32[]{:S(2)}) async-start(), calls=%async_computation.4 | async-start | bytes 4718592 | tf_op jit(solution)/shard_map/psum | solution.py:50
  221.0 222.4 %all-reduce.12.cloned.1.call-start = ((), (), s32[]{:S(2)}) async-start(), calls=%async_computation.2 | async-start | bytes 524288 | tf_op jit(solution)/shard_map/psum | solution.py:12
  357.3 62.1 %copy-start = (f32[256,2048]{1,0:T(8,128)S(1)}, f32[256,2048]{1,0:T(8,128)}, u32[]{:S(2)}) copy-start(f32[256,2048]{1,0:T(8,128)} %get-tuple-element.38) | copy-start | bytes 6291460
  357.3 62.1 %copy-start.4 = (f32[256,256]{0,1:T(8,128)S(1)}, f32[256,256]{0,1:T(8,128)}, u32[]{:S(2)}) copy-start(f32[256,256]{0,1:T(8,128)} %all-reduce.10.cloned.1.call-done) | copy-start | bytes 786436
  422.9 1.3 copy-start.2
  425.4 150.9 %all-reduce.14.cloned.1.call-start = ((), (), s32[]{:S(2)}) async-start(), calls=%async_computation.3 | async-start | bytes 4194304 | tf_op jit(solution)/shard_map/psum | solution.py:58
  448.3 1.5 copy-start.6
  450.0 3.1 copy-start.5
  576.3 1.4 slice-start
  577.7 2.2 copy-start.3
Sparse Core Ops, SparseCore 0:
  13.8 107.7 all-reduce.7
  195.2 21.5 all-reduce.9
  222.9 132.4 all-reduce.15
  425.5 17.8 all-reduce.11
  448.7 127.5 all-reduce.13
where the time goes:
time: 598 us; the launch traced here: 589 us
  waiting for transfers between devices  407 us (68%)
  other arithmetic  117 us (20%)
  matrix products  23.2 us (4%)
  between operations  17 us (3%)
  local copies, waits for them, and re-layouts  13.6 us (2%)
  loops' own time  12 us (2%)
    psum x1, waiting for transfers between devices, body(): lax.psum((local_terms, inner(second_panel, second_panel)), 'row')  134 us
    psum x1, waiting for transfers between devices, body(): second_proj = lax.psum(inner(basis_second, remainder), 'row')  122 us
    psum x1, waiting for transfers between devices, body(): first_gram = lax.psum(inner(first_panel, first_panel), 'row')  112 us
    another operation x13, other arithmetic, factor(): lower_factor = jnp.linalg.cholesky(safe_gram)  68.5 us
    another operation x3, other arithmetic, factor(): lax.linalg.triangular_solve(lower_factor, identity, left_side=True, lower...  39.4 us
    psum x2, waiting for transfers between devices, spread(): return lax.psum(kept, axis)  38.3 us
    dot_general x5, matrix products, inner(): lax.dot_general(left, right, (((0,), (0,)), ((), ())), precision=lax.Prec...  14.4 us
    another operation x2, loops' own time, factor(): lax.linalg.triangular_solve(lower_factor, identity, left_side=True, lower...  12 us
  transfers between devices with their start and end apart: 5, of which 5 were waited for; matrix products, arithmetic and copies ran while one was open for 1% of the time, Pallas kernels for 0%

commit v1 on v0

--- a/solution.py
+++ b/solution.py
@@ -42,7 +42,7 @@
     panels = matrix[:, : 2 * panel_cols]
     first_panel = panels[:, :panel_cols]
     second_panel = panels[:, panel_cols:]
-    first_gram = lax.psum(inner(first_panel, first_panel), "row")
+    first_gram = jnp.sum(lax.all_gather(inner(first_panel, first_panel), "row"), axis=0)
     upper_first, inverse_first = factor(first_gram, holder)
     basis_first = product(first_panel, inverse_first)
     basis_first = spread(basis_first, "col", 0)

time: 598 us -> 564 us (0.943)
  waiting for transfers between devices: 407 us -> 370 us
    psum x1 -> x0, waiting for transfers between devices: 112 us -> none  [body(): first_gram = lax.psum(inner(first_panel, first_panel), 'row')]
    all_gather x0 -> x1, waiting for transfers between devices: none -> 77.7 us  [body(): lax.all_gather(inner(first_panel, first_panel), 'row')]
where the time goes in v1:
time: 564 us; the launch traced here: 555 us
  waiting for transfers between devices  370 us (66%)
  other arithmetic  119 us (21%)
  matrix products  23.2 us (4%)
  between operations  17 us (3%)
  local copies, waits for them, and re-layouts  13.8 us (2%)
  loops' own time  12 us (2%)
    psum x1, waiting for transfers between devices, body(): lax.psum((local_terms, inner(second_panel, second_panel)), 'row')  134 us
    psum x1, waiting for transfers between devices, body(): second_proj = lax.psum(inner(basis_second, remainder), 'row')  122 us
    all_gather x1, waiting for transfers between devices, body(): lax.all_gather(inner(first_panel, first_panel), 'row')  77.7 us
    another operation x13, other arithmetic, factor(): lower_factor = jnp.linalg.cholesky(safe_gram)  68.5 us
    another operation x3, other arithmetic, factor(): lax.linalg.triangular_solve(lower_factor, identity, left_side=True, lower...  39.4 us
    psum x2, waiting for transfers between devices, spread(): return lax.psum(kept, axis)  35.6 us
    dot_general x5, matrix products, inner(): lax.dot_general(left, right, (((0,), (0,)), ((), ())), precision=lax.Prec...  14.4 us
    another operation x2, loops' own time, factor(): lax.linalg.triangular_solve(lower_factor, identity, left_side=True, lower...  12 us
  transfers between devices with their start and end apart: 5, of which 5 were waited for; matrix products, arithmetic and copies ran while one was open for 1% of the time, Pallas kernels for 0%

profile of v1, /device:TPU:1, one launch (start us, length us, event | category | flops | bytes accessed | tf_op | source)
XLA Modules:
  0.0 555.1 jit_solution(935020550156337219)
XLA Ops:
  7.2 2.3 fusion.18
  9.6 0.0 all-reduce.7.cloned.1.call-start
  9.7 77.7 %all-gather.3.cloned.1.call-done = f32[4096,256]{1,0:T(8,128)} async-done(((f32[256,256]{1,0:T(8,128)}), f32[4096,256]{1,0:T(8,128)}) %all-gather.3.cloned.1.call-update) | async-done | bytes 4194320 | tf_op jit(solution)/shard_map/all_gather | solution.py:45
  87.4 2.5 reduce_sum.9
  89.8 0.1 copy.13
  90.0 0.1 copy.14
  90.2 11.7 %cholesky.130 = f32[128,128]{1,0:T(8,128)S(1)} custom-call(f32[128,128]{1,0:T(8,128)S(1)} %cholesky.194), custom_call_target="Cholesky" | custom-call | tf_op jit(solution)/shard_map/jit(cholesky)/cholesky | solution.py:33
  102.0 9.8 %custom-call.13 = f32[1,128,128]{1,2,0:T(8,128)S(1)} custom-call(f32[1,128,128]{2,1,0:T(8,128)S(1)} %get-tuple-element.57), custom_call_target="InvertDiagBlocksLowerTriangular" | custom-call | tf_op jit(solution)/shard_map/jit(cholesky)/cholesky | solution.py:33
  111.8 0.2 constant_dynamic-update-slice_fusion.3
  112.0 0.3 convolution_subtract_fusion.5
  112.3 11.7 %cholesky.147 = f32[128,128]{1,0:T(8,128)S(1)} custom-call(f32[128,128]{1,0:T(8,128)S(1)} %convolution_subtract_fusion.5), custom_call_target="Cholesky" | custom-call | tf_op jit(solution)/shard_map/jit(cholesky)/cholesky | solution.py:33
  124.1 0.6 compare_reduce_fusion.2
  126.0 0.1 broadcast.93
  126.0 15.5 %while.4 = (s32[]{:T(128)}, f32[256,256]{1,0:T(8,128)S(1)}, s32[2,2]{1,0:T(2,128)S(1)}, f32[2,128,128]{2,1,0:T(8,128)S(1)}, s32[]{:T(128)}) while((s32[]{:T(128)}, f32[256,256]{1,0:T(8,128)S(1)}, s32[2,2]{1,0:T(2,128)S(1)}, f32[2,128,128]{2,1,0:T(8,128)S(1)}, s32[]{:T(128)}) %tuple.51), condition=%wide.while_cond, body=%wide.while_body.sunk | while | flops 2 | bytes 131189 | solution.py:34
  137.8 0.6 fusion.59
  138.4 1.3 bitcast_dynamic-update-slice_fusion.4
  139.7 0.6 fusion.59
  140.3 1.3 bitcast_dynamic-update-slice_fusion.4
  141.6 19.7 %custom-call.14 = f32[2,128,128]{1,2,0:T(8,128)S(1)} custom-call(f32[2,128,128]{2,1,0:T(8,128)S(1)} %get-tuple-element.18), custom_call_target="InvertDiagBlocksLowerTriangular" | custom-call | tf_op jit(solution)/shard_map/triangular_solve/custom-call.0 | solution.py:34
  161.3 0.3 fusion.25
  161.6 0.4 convolution_subtract_fusion.3
  162.0 0.3 fusion.32
  162.3 1.1 fusion.1
  163.5 0.0 all-reduce.13.cloned.1.call-start
  163.5 1.3 fusion.14
  164.8 17.7 %all-reduce.7.cloned.1.call-done = f32[256,256]{0,1:T(8,128)} async-done(((f32[256,256]{0,1:T(8,128)}), f32[256,256]{0,1:T(8,128)}) %all-reduce.7.cloned.1.call-update) | async-done | bytes 262160 | tf_op jit(solution)/shard_map/psum | solution.py:12
  182.5 4.2 fusion.41
  186.7 0.0 all-reduce.9.cloned.1.call-start
  186.7 134.4 %all-reduce.13.cloned.1.call-done = (f32[256,2048]{1,0:T(8,128)}, f32[256,256]{0,1:T(8,128)}) async-done(((f32[256,2048]{1,0:T(8,128)}, f32[256,256]{0,1:T(8,128)}), (f32[256,2048]{1,0:T(8,128)}, f32[256,256]{0,1:T(8,128)})) %all-reduce.13.cloned.1.call-update) | async-done | bytes 2359312 | tf_op jit(solution)/shard_map/psum | solution.py:50
  321.1 1.7 fusion
  322.9 0.1 copy.19
  323.1 11.7 %cholesky.164 = f32[128,128]{1,0:T(8,128)S(1)} custom-call(f32[128,128]{1,0:T(8,128)S(1)} %cholesky.197), custom_call_target="Cholesky" | custom-call | tf_op jit(solution)/shard_map/jit(cholesky)/cholesky | solution.py:33
  334.8 0.6 compare_reduce_fusion.1
  335.5 9.8 %custom-call.15 = f32[1,128,128]{1,2,0:T(8,128)S(1)} custom-call(f32[1,128,128]{2,1,0:T(8,128)S(1)} %get-tuple-element.53), custom_call_target="InvertDiagBlocksLowerTriangular" | custom-call | tf_op jit(solution)/shard_map/jit(cholesky)/cholesky | solution.py:33
  345.3 0.2 constant_dynamic-update-slice_fusion.1
  345.5 0.3 convolution_subtract_fusion.4
  345.8 11.7 %cholesky.181 = f32[128,128]{1,0:T(8,128)S(1)} custom-call(f32[128,128]{1,0:T(8,128)S(1)} %convolution_subtract_fusion.4), custom_call_target="Cholesky" | custom-call | tf_op jit(solution)/shard_map/jit(cholesky)/cholesky | solution.py:33
  357.5 0.6 compare_reduce_fusion
  359.5 0.7 fusion.22
  360.2 4.1 while.5
  360.4 0.6 fusion.60
  361.0 1.4 bitcast_dynamic-update-slice_fusion.5
  362.4 0.6 fusion.60
  363.0 1.4 bitcast_dynamic-update-slice_fusion.5
  364.4 19.7 %custom-call.16 = f32[2,128,128]{1,2,0:T(8,128)S(1)} custom-call(f32[2,128,128]{2,1,0:T(8,128)S(1)} %get-tuple-element.19), custom_call_target="InvertDiagBlocksLowerTriangular" | custom-call | tf_op jit(solution)/shard_map/triangular_solve/custom-call.0 | solution.py:34
  384.1 0.3 fusion.23
  384.4 0.4 convolution_subtract_fusion.2
  384.8 0.3 fusion.28
  385.1 3.5 convolution_subtract_fusion
  388.7 1.3 copy-done.2
  390.0 1.1 convolution_select_fusion
  391.1 0.0 all-reduce.11.cloned.1.call-start
  391.2 18.0 %all-reduce.9.cloned.1.call-done = f32[256,256]{0,1:T(8,128)} async-done(((f32[256,256]{0,1:T(8,128)}), f32[256,256]{0,1:T(8,128)}) %all-reduce.9.cloned.1.call-update) | async-done | bytes 262160 | tf_op jit(solution)/shard_map/psum | solution.py:12
  409.2 4.9 fusion.42
  414.1 0.1 copy.16
  414.2 1.4 slice.98
  415.6 0.1 copy.22
  415.7 3.1 maximum_select_fusion
  418.9 1.0 copy.23
  419.9 122.1 %all-reduce.11.cloned.1.call-done = f32[256,2048]{1,0:T(8,128)} async-done(((f32[256,2048]{1,0:T(8,128)}), f32[256,2048]{1,0:T(8,128)}) %all-reduce.11.cloned.1.call-update) | async-done | bytes 2097168 | tf_op jit(solution)/shard_map/psum | solution.py:58
  542.0 1.4 slice-done
  543.4 2.0 maximum_select_fusion.1
  545.5 0.2 copy-done.3
  545.6 2.5 pad_maximum_fusion
  (41 shorter events, 0.6 us)
Async XLA Ops:
  7.2 80.2 %all-gather.3.cloned.1.call-start = ((), (), s32[]{:S(2)}) async-start(), calls=%async_computation.3 | async-start | bytes 4456448 | tf_op jit(solution)/shard_map/all_gather | solution.py:45
  9.6 172.9 %all-reduce.7.cloned.1.call-start = ((), (), s32[]{:S(2)}) async-start(), calls=%async_computation | async-start | bytes 524288 | tf_op jit(solution)/shard_map/psum | solution.py:12
  90.2 72.1 %copy-start.1 = (f32[256,2048]{1,0:T(8,128)S(1)}, f32[256,2048]{1,0:T(8,128)}, u32[]{:S(2)}) copy-start(f32[256,2048]{1,0:T(8,128)} %param.4) | copy-start | bytes 6291460
  163.5 157.7 %all-reduce.13.cloned.1.call-start = ((), (), s32[]{:S(2)}) async-start(), calls=%async_computation.4 | async-start | bytes 4718592 | tf_op jit(solution)/shard_map/psum | solution.py:50
  186.7 222.5 %all-reduce.9.cloned.1.call-start = ((), (), s32[]{:S(2)}) async-start(), calls=%async_computation.1 | async-start | bytes 524288 | tf_op jit(solution)/shard_map/psum | solution.py:12
  323.0 62.1 %copy-start = (f32[256,2048]{1,0:T(8,128)S(1)}, f32[256,2048]{1,0:T(8,128)}, u32[]{:S(2)}) copy-start(f32[256,2048]{1,0:T(8,128)} %get-tuple-element.40) | copy-start | bytes 6291460
  323.1 62.1 %copy-start.4 = (f32[256,256]{0,1:T(8,128)S(1)}, f32[256,256]{0,1:T(8,128)}, u32[]{:S(2)}) copy-start(f32[256,256]{0,1:T(8,128)} %all-reduce.7.cloned.1.call-done) | copy-start | bytes 786436
  388.7 1.3 copy-start.2
  391.1 150.9 %all-reduce.11.cloned.1.call-start = ((), (), s32[]{:S(2)}) async-start(), calls=%async_computation.2 | async-start | bytes 4194304 | tf_op jit(solution)/shard_map/psum | solution.py:58
  414.1 1.5 copy-start.6
  415.7 3.1 copy-start.5
  542.0 1.4 slice-start
  543.4 2.2 copy-start.3
Sparse Core Ops, SparseCore 0:
  11.3 76.0 all-gather.2
  163.6 18.8 all-reduce.6
  188.6 132.4 all-reduce.12
  391.2 17.8 all-reduce.8
  414.5 127.4 all-reduce.10
